TPU v7x, 512 devices: a whole 4x4x16 slice. The times are simulated.
512 devices in a mesh: dp: 32 (over z, y_lo), tensor: 16 (over y_hi, x, core).
Axes of the slice: x: 4, y: 4 (y_hi: 2, y_lo: 2; y = y_hi * 2 + y_lo), z: 16, core: 2. Of those that a mesh axis runs over, the one named last changes fastest.
Arguments:
- activations: bfloat16 [32768, 8192], P('dp', 'tensor'), may hold values from -6 to 6
- out_grads: bfloat16 [32768, 8192], P('dp', 'tensor'), may hold values from -6 to 6
- proj_in: bfloat16 [8192, 64], P('tensor'), may hold values from -0.0625 to 0.0625
- proj_out: bfloat16 [8192, 64], P('tensor'), may hold values from -0.0625 to 0.0625
- segment_ids: int32 [32, 1024], P('dp'), may hold values from 0 to 23, never falling along the last dimension, each value on 1 to 80 neighbouring positions
- train_logs: bfloat16 [131072, 4096], P('dp', 'tensor'), may hold values from -6 to 6
- doc_ids: int32 [131072], P(('dp', 'tensor')), may hold values from 0 to 255
Outputs:
- scores: float32 [768, 131072], P(None, ('dp', 'tensor'))
- doc_influence: float32 [768, 256], replicated
Inputs may be any that keep to these rules, and one draw needn't show every extreme that they name: `segment_ids`: in each row the example numbers never fall; each of the 24 examples has 1 to 80 tokens, and one has exactly 80.
All inputs are finite; a program needn't handle non-finite values.
Results may differ from a plain program's by a relative error of at most 0.0052.
Values may be sent and summed in bfloat16 or wider, within the bound.
No kernel may reach another device: no remote copies, remote signals or barrier semaphores. Data moves between devices by JAX's collectives and lax.ppermute only.
A program may use at most 64 MiB of HBM per device.

v0:
```python
import math
import jax
import jax.numpy as jnp
from jax import lax
from jax.sharding import PartitionSpec as P

EX_DEV = 24
DOCS = 256


def per_device(activations, out_grads, proj_in, proj_out, segment_ids, train_logs, doc_ids):
    width_parts = lax.axis_size("tensor")
    position = lax.axis_index("tensor")
    tok_rows = activations.shape[0]
    rank = proj_in.shape[1]
    partial_value = jnp.concatenate(
        [
            jnp.dot(activations, proj_in, preferred_element_type=jnp.float32),
            jnp.dot(out_grads, proj_out, preferred_element_type=jnp.float32),
        ],
        axis=1,
    )
    seg_row = segment_ids[0]
    labels = jnp.arange(EX_DEV, dtype=jnp.int32)
    counts = jnp.sum((seg_row[:, None] == labels[None, :]).astype(jnp.float32), axis=0)
    block_rank = rank // width_parts
    summed = lax.psum(partial_value, "tensor").astype(jnp.bfloat16)
    in_proj = summed[:, :rank]
    out_proj = summed[:, rank:]
    own_out = lax.dynamic_slice_in_dim(out_proj, position * block_rank, block_rank, 1)
    member = (seg_row[:, None] == labels[None, :]).astype(jnp.bfloat16)
    masked = (member[:, :, None] * own_out[:, None, :]).reshape(tok_rows, EX_DEV * block_rank)
    log_sums = jnp.einsum("ta,tj->aj", masked, in_proj, preferred_element_type=jnp.float32)
    log_sums = log_sums.reshape(EX_DEV, block_rank * rank)
    query_block = (log_sums / counts[:, None]).astype(jnp.bfloat16)
    train_full = lax.all_to_all(train_logs, "tensor", split_axis=0, concat_axis=1, tiled=True)
    local_rows = train_full.shape[0]
    wide_block = lax.all_gather(query_block, "tensor", axis=1, tiled=True)
    rows = lax.dot_general(
        lax.all_gather(wide_block, "dp", axis=0, tiled=True),
        train_full,
        (((1,), (1,)), ((), ())),
        preferred_element_type=jnp.float32,
    )
    scores = rows * 0.125
    doc_labels = jnp.arange(DOCS, dtype=jnp.int32)
    doc_hot = (doc_ids[:, None] == doc_labels[None, :]).astype(jnp.float32)
    doc_part = jnp.dot(scores, doc_hot, precision=lax.Precision.HIGHEST)
    total_rows = local_rows * lax.axis_size("tensor") * lax.axis_size("dp")
    doc_total = lax.psum(doc_part, ("dp", "tensor"))
    doc_influence = doc_total / math.sqrt(total_rows / DOCS)
    return (scores, doc_influence)


def solution(mesh):
    placed = (
        P("dp", "tensor"),
        P("dp", "tensor"),
        P("tensor", None),
        P("tensor", None),
        P("dp", None),
        P("dp", "tensor"),
        P(("dp", "tensor")),
    )
    return jax.shard_map(
        per_device,
        mesh=mesh,
        in_specs=placed,
        out_specs=(P(None, ("dp", "tensor")), P()),
        check_vma=False,
    )
```

profile of v0, /device:TPU:2, one launch (start us, length us, event | category | flops | bytes accessed | tf_op | source)
XLA Modules:
  0.0 761.5 jit_solution(6124716450737580398)
XLA Ops:
  7.2 0.0 copy-start
  7.2 0.0 all-gather.2.cloned.1.call-start
  7.2 0.9 convert_reduce_fusion
  8.1 0.7 fusion.4
  8.8 0.0 copy-done
  8.8 1.3 fusion.5
  10.1 1.7 fusion.6
  11.8 0.1 pad_maximum_fusion
  11.8 70.0 %all-reduce.4 = bf16[1024,128]{0,1:T(8,128)(2,1)S(1)} all-reduce(f32[1024,128]{0,1:T(8,128)S(1)} %pad_maximum_fusion), channel_id=1, replica_groups=mesh['dp'=32,'tensor'=16] {'tensor'}, use_global_device_ids=true, to_apply=%region_0.0 | all-reduce | flops 131072 | bytes 786432 | tf_op jit(solution)/shard_map/psum | solution.py:27
  81.9 0.1 broadcast_multiply_fusion.1
  82.0 0.1 mul.30
  82.0 0.2 fusion.1
  82.2 0.1 reshape.42
  82.3 0.1 divide_convert_fusion
  82.4 27.0 %all_gather.6 = bf16[24,4096]{1,0:T(8,128)(2,1)} all-gather(bf16[24,256]{1,0:T(8,128)(2,1)S(1)} %divide_convert_fusion), channel_id=1, replica_groups=mesh['dp'=32,'tensor'=16] {'tensor'}, dimensions={1}, use_global_device_ids=true | all-gather | bytes 208896 | tf_op jit(solution)/shard_map/all_gather | solution.py:38
  109.4 0.0 all-gather.2.cloned.1.call-update
  109.4 0.0 all-reduce.3.cloned.1.call-start
  109.4 34.0 %all_to_all.19 = bf16[16,256,256]{2,1,0:T(8,128)(2,1)S(1)} all-to-all(bf16[16,256,256]{2,1,0:T(8,128)(2,1)} %bitcast.15), channel_id=1, replica_groups=mesh['dp'=32,'tensor'=16] {'tensor'}, dimensions={0} | all-to-all | bytes 4194304 | tf_op jit(solution)/shard_map/all_to_all | solution.py:36
  143.5 2.4 copy.12
  145.9 133.8 %all-gather.2.cloned.1.call-done = bf16[768,4096]{1,0:T(8,128)(2,1)} async-done(((bf16[24,4096]{1,0:T(8,128)(2,1)}), bf16[768,4096]{1,0:T(8,128)(2,1)}) %all-gather.2.cloned.1.call-update) | async-done | bytes 6291472 | tf_op jit(solution)/shard_map/all_gather | solution.py:40
  279.7 0.0 copy-start.2
  279.7 5.2 convolution_multiply_fusion
  284.9 0.0 copy-done.2
  284.9 0.0 copy-start.1
  284.9 1.5 fusion
  286.4 0.0 all-reduce.3.cloned.1.call-update
  286.4 466.2 %all-reduce.3.cloned.1.call-done = f32[768,256]{1,0:T(8,128)} async-done(((f32[768,256]{1,0:T(8,128)}), f32[768,256]{1,0:T(8,128)}) %all-reduce.3.cloned.1.call-update) | async-done | bytes 786448 | tf_op jit(solution)/shard_map/psum | solution.py:50
  752.6 2.1 broadcast_multiply_fusion
  754.7 0.0 copy-done.1
  (2 shorter events, 0.0 us)
Async XLA Ops:
  7.2 1.7 copy-start
  7.2 272.5 %all-gather.2.cloned.1.call-start = ((), (), s32[]{:S(2)}) async-start(), calls=%async_computation.1 | async-start | bytes 6488064 | tf_op jit(solution)/shard_map/all_gather | solution.py:40
  109.4 643.2 %all-reduce.3.cloned.1.call-start = ((), (), s32[]{:S(2)}) async-start(), calls=%async_computation.2 | async-start | bytes 1572864 | tf_op jit(solution)/shard_map/psum | solution.py:50
  279.7 5.2 copy-start.2
  284.9 469.8 %copy-start.1 = (f32[768,256]{1,0:T(8,128)}, f32[768,256]{1,0:T(8,128)S(1)}, u32[]{:S(2)}) copy-start(f32[768,256]{1,0:T(8,128)S(1)} %convolution_multiply_fusion) | copy-start | bytes 2359300
Sparse Core Ops, SparseCore 0:
  109.5 170.1 all-gather.1
  286.5 466.0 all-reduce.2
where the time goes:
time: 762 us
  waiting for transfers between devices  600 us (79%)
  blocking collectives  131 us (17%)
  between operations  14.1 us (2%)
  matrix products  9.8 us (1%)
    psum x1, waiting for transfers between devices, per_device(): doc_total = lax.psum(doc_part, ('dp', 'tensor'))  466 us
    all_gather x1, waiting for transfers between devices, per_device(): lax.all_gather(wide_block, 'dp', axis=0, tiled=True)  134 us
    psum x1, blocking collectives, per_device(): summed = lax.psum(partial_value, 'tensor').astype(jnp.bfloat16)  70 us
    all_to_all x1, blocking collectives, per_device(): lax.all_to_all(train_logs, 'tensor', split_axis=0, concat_axis=1, tiled=T...  34 us
    all_gather x1, blocking collectives, per_device(): wide_block = lax.all_gather(query_block, 'tensor', axis=1, tiled=True)  27 us
  transfers between devices with their start and end apart: 2, of which 2 were waited for; matrix products, arithmetic and copies ran while one was open for 0% of the time, Pallas kernels for 0%

commit v1 on v0

--- a/solution.py
+++ b/solution.py
@@ -3,6 +3,7 @@
 import jax.numpy as jnp
 from jax import lax
 from jax.sharding import PartitionSpec as P
+from jax.lax import psum
 
 EX_DEV = 24
 DOCS = 256
@@ -47,7 +48,8 @@
     doc_hot = (doc_ids[:, None] == doc_labels[None, :]).astype(jnp.float32)
     doc_part = jnp.dot(scores, doc_hot, precision=lax.Precision.HIGHEST)
     total_rows = local_rows * lax.axis_size("tensor") * lax.axis_size("dp")
-    doc_total = lax.psum(doc_part, ("dp", "tensor"))
+    y_new = psum(doc_part, axis_name="dp")
+    doc_total = psum(y_new, axis_name="tensor")
     doc_influence = doc_total / math.sqrt(total_rows / DOCS)
     return (scores, doc_influence)
 

time: 762 us -> 715 us (0.938)
  the two profiles are of different devices: /device:TPU:2 before, /device:TPU:1 now
where the time goes in v1:
time: 715 us
  waiting for transfers between devices  553 us (77%)
  blocking collectives  132 us (18%)
  between operations  13.8 us (2%)
  matrix products  9.8 us (1%)
    psum x1, waiting for transfers between devices, per_device(): y_new = psum(doc_part, axis_name='dp')  245 us
    psum x1, waiting for transfers between devices, per_device(): doc_total = psum(y_new, axis_name='tensor')  178 us
    all_gather x1, waiting for transfers between devices, per_device(): lax.all_gather(wide_block, 'dp', axis=0, tiled=True)  130 us
    psum x1, blocking collectives, per_device(): summed = lax.psum(partial_value, 'tensor').astype(jnp.bfloat16)  71 us
    all_to_all x1, blocking collectives, per_device(): lax.all_to_all(train_logs, 'tensor', split_axis=0, concat_axis=1, tiled=T...  33.9 us
    all_gather x1, blocking collectives, per_device(): wide_block = lax.all_gather(query_block, 'tensor', axis=1, tiled=True)  26.8 us
  transfers between devices with their start and end apart: 3, of which 3 were waited for; matrix products, arithmetic and copies ran while one was open for 0% of the time, Pallas kernels for 0%

profile of v1, /device:TPU:1, one launch (start us, length us, event | category | flops | bytes accessed | tf_op | source)
XLA Modules:
  0.0 714.6 jit_solution(17143630948562208611)
XLA Ops:
  7.2 0.0 copy-start
  7.2 0.0 all-gather.2.cloned.1.call-start
  7.2 0.9 convert_reduce_fusion
  8.1 0.7 fusion.4
  8.8 0.0 copy-done
  8.8 1.3 fusion.5
  10.1 1.7 fusion.6
  11.8 0.1 pad_maximum_fusion
  11.8 71.0 %all-reduce.7 = bf16[1024,128]{0,1:T(8,128)(2,1)S(1)} all-reduce(f32[1024,128]{0,1:T(8,128)S(1)} %pad_maximum_fusion), channel_id=1, replica_groups=mesh['dp'=32,'tensor'=16] {'tensor'}, use_global_device_ids=true, to_apply=%region_0.0 | all-reduce | flops 131072 | bytes 786432 | tf_op jit(solution)/shard_map/psum | solution.py:28
  82.9 0.1 broadcast_multiply_fusion.1
  83.0 0.1 mul.30
  83.0 0.2 fusion.1
  83.2 0.1 reshape.42
  83.3 0.1 divide_convert_fusion
  83.4 26.8 %all_gather.6 = bf16[24,4096]{1,0:T(8,128)(2,1)} all-gather(bf16[24,256]{1,0:T(8,128)(2,1)S(1)} %divide_convert_fusion), channel_id=1, replica_groups=mesh['dp'=32,'tensor'=16] {'tensor'}, dimensions={1}, use_global_device_ids=true | all-gather | bytes 208896 | tf_op jit(solution)/shard_map/all_gather | solution.py:39
  110.2 0.0 all-gather.2.cloned.1.call-update
  110.2 0.0 all-reduce.4.cloned.1.call-start
  110.3 33.9 %all_to_all.19 = bf16[16,256,256]{2,1,0:T(8,128)(2,1)S(1)} all-to-all(bf16[16,256,256]{2,1,0:T(8,128)(2,1)} %bitcast.15), channel_id=1, replica_groups=mesh['dp'=32,'tensor'=16] {'tensor'}, dimensions={0} | all-to-all | bytes 4194304 | tf_op jit(solution)/shard_map/all_to_all | solution.py:37
  144.2 2.4 copy.12
  146.6 129.9 %all-gather.2.cloned.1.call-done = bf16[768,4096]{1,0:T(8,128)(2,1)} async-done(((bf16[24,4096]{1,0:T(8,128)(2,1)}), bf16[768,4096]{1,0:T(8,128)(2,1)}) %all-gather.2.cloned.1.call-update) | async-done | bytes 6291472 | tf_op jit(solution)/shard_map/all_gather | solution.py:41
  276.5 0.0 copy-start.2
  276.5 5.2 convolution_multiply_fusion
  281.7 0.0 copy-done.2
  281.7 0.0 copy-start.1
  281.7 1.5 fusion
  283.2 0.0 all-reduce.4.cloned.1.call-update
  283.2 0.0 all-reduce.6.cloned.1.call-start
  283.3 245.1 %all-reduce.4.cloned.1.call-done = f32[768,256]{1,0:T(8,128)} async-done(((f32[768,256]{1,0:T(8,128)}), f32[768,256]{1,0:T(8,128)}) %all-reduce.4.cloned.1.call-update) | async-done | bytes 786448 | tf_op jit(solution)/shard_map/psum | solution.py:51
  528.3 0.0 all-reduce.6.cloned.1.call-update
  528.3 177.7 %all-reduce.6.cloned.1.call-done = f32[768,256]{1,0:T(8,128)} async-done(((f32[768,256]{1,0:T(8,128)}), f32[768,256]{1,0:T(8,128)}) %all-reduce.6.cloned.1.call-update) | async-done | bytes 786448 | tf_op jit(solution)/shard_map/psum | solution.py:52
  706.0 2.1 broadcast_multiply_fusion
  708.1 0.0 copy-done.1
  (2 shorter events, 0.0 us)
Async XLA Ops:
  7.2 1.7 copy-start
  7.2 269.3 %all-gather.2.cloned.1.call-start = ((), (), s32[]{:S(2)}) async-start(), calls=%async_computation.1 | async-start | bytes 6488064 | tf_op jit(solution)/shard_map/all_gather | solution.py:41
  110.2 418.1 %all-reduce.4.cloned.1.call-start = ((), (), s32[]{:S(2)}) async-start(), calls=%async_computation.2 | async-start | bytes 1572864 | tf_op jit(solution)/shard_map/psum | solution.py:51
  276.5 5.2 copy-start.2
  281.7 426.4 %copy-start.1 = (f32[768,256]{1,0:T(8,128)}, f32[768,256]{1,0:T(8,128)S(1)}, u32[]{:S(2)}) copy-start(f32[768,256]{1,0:T(8,128)S(1)} %convolution_multiply_fusion) | copy-start | bytes 2359300
  283.2 422.8 %all-reduce.6.cloned.1.call-start = ((), (), s32[]{:S(2)}) async-start(), calls=%async_computation.3 | async-start | bytes 1572864 | tf_op jit(solution)/shard_map/psum | solution.py:52
Sparse Core Ops, SparseCore 0:
  110.4 166.0 all-gather.1
  283.3 244.9 all-reduce.3
  531.5 174.4 all-reduce.5
